TPU v7x, 32 devices: a whole 2x2x4 slice. The times are simulated.
32 devices in a mesh: dp: 8 (over z, x), seq: 4 (over y, core).
Axes of the slice: x: 2, y: 2, z: 4, core: 2. Of those that a mesh axis runs over, the one named last changes fastest.
Arguments:
- enc_rows: bfloat16 [32, 256, 1280], P('dp', 'seq'), may hold values from -100 to 100
- out_weight: bfloat16 [1280, 512], replicated, may hold values from -3 to 3
- labels: int32 [32, 63], P('dp'), may hold values from 1 to 511
- label_count: int32 [32], P('dp'), may hold values from 1 to 63, as said below
- frame_count: int32 [32], P('dp'), may hold values from 128 to 256, as said below
Outputs:
- logit_grad: bfloat16 [32, 256, 512], P('dp', 'seq')
- row_grad: bfloat16 [32, 256, 1280], P('dp', 'seq')
- weight_grad: float32 [1280, 512], P('dp', 'seq')
Inputs may be any that keep to these rules, and one draw needn't show every extreme that they name: `labels`: character ids; id 0 is the blank and never appears. `label_count`: some utterance has 63 labels in every draw. `frame_count`: some utterance has 256 frames in every draw.
All inputs are finite; a program needn't handle non-finite values.
Results may differ from a plain program's by a relative error of at most 0.0043.
Values sent between devices are 32-bit elements; how exact they have to be, the bound alone decides.
A program may use at most 64 MiB of HBM per device.

v0:
```python
import jax
import jax.numpy as jnp
from jax import lax
from jax.sharding import PartitionSpec as P

negative_fill = -1e30


def from_behind(block, axis, distance):
    devices = range(lax.axis_size(axis))
    route = [(i - distance, i) for i in devices if i - distance in devices]
    return lax.ppermute(block, axis, route)


def merge_three(first_term, second_term, third_term):
    highest = jnp.maximum(jnp.maximum(first_term, second_term), third_term)
    return highest + jnp.log(
        jnp.exp(first_term - highest)
        + jnp.exp(second_term - highest)
        + jnp.exp(third_term - highest)
    )


def shift_right(values, amount):
    filler = jnp.full((values.shape[0], amount), negative_fill, jnp.float32)
    return jnp.concatenate([filler, values[:, :-amount]], axis=1)


def shift_left(values, amount):
    filler = jnp.full((values.shape[0], amount), negative_fill, jnp.float32)
    return jnp.concatenate([values[:, amount:], filler], axis=1)


def advance(current, emission, usable, allowed):
    from_one = shift_right(current, 1)
    from_two = jnp.where(allowed, shift_right(current, 2), negative_fill)
    fresh = merge_three(current, from_one, from_two) + emission
    return jnp.where(usable[:, None], fresh, current)


def retreat(current, emission, usable, allowed_next):
    summed = current + emission
    next_one = shift_left(summed, 1)
    next_two = jnp.where(allowed_next, shift_left(summed, 2), negative_fill)
    fresh = merge_three(summed, next_one, next_two)
    return jnp.where(usable[:, None], fresh, current)


def lattice(labels, label_count):
    utterances, length = labels.shape
    states_wide = 2 * length + 2
    blanks = jnp.zeros((utterances, length + 1), jnp.int32)
    chars = jnp.concatenate([labels, jnp.full((utterances, 1), -1, jnp.int32)], axis=1)
    extended = jnp.stack([blanks, chars], axis=2).reshape(utterances, states_wide)
    earlier = jnp.concatenate([jnp.full((utterances, 2), -2, jnp.int32), extended[:, :-2]], axis=1)
    positions = jnp.arange(states_wide, dtype=jnp.int32)[None, :]
    allowed = (positions % 2 == 1) & (positions >= 3) & (extended != earlier)
    allowed_next = jnp.concatenate([allowed[:, 2:], jnp.zeros((utterances, 2), jnp.bool_)], axis=1)
    zeros_row = jnp.zeros((utterances, states_wide), jnp.float32)
    initial = jnp.where(positions == 0, zeros_row, negative_fill)
    doubled = 2 * label_count[:, None]
    closing = jnp.where(
        (positions == doubled) | (positions == doubled - 1), zeros_row, negative_fill
    )
    return (allowed, allowed_next, initial, closing)


def emissions(logprob, labels):
    utterances, frames, vocabulary = logprob.shape
    length = labels.shape[1]
    char_index = jnp.concatenate([jnp.zeros((utterances, 1), jnp.int32), labels], axis=1)
    picked = jnp.take_along_axis(
        logprob, jnp.broadcast_to(char_index[:, None, :], (utterances, frames, length + 1)), axis=2
    )
    blank_part = jnp.broadcast_to(picked[:, :, :1], picked.shape)
    label_part = jnp.concatenate(
        [picked[:, :, 1:], jnp.full((utterances, frames, 1), negative_fill, jnp.float32)], axis=2
    )
    emission = jnp.stack([blank_part, label_part], axis=3).reshape(
        utterances, frames, 2 * length + 2
    )
    return (jnp.swapaxes(emission, 0, 1), char_index)


def forward_pass(initial, emission, usable, allowed):

    def frame_step(current, inputs):
        fresh = advance(current, inputs[0], inputs[1], allowed)
        return (fresh, fresh)

    return lax.scan(frame_step, initial, (emission, usable), unroll=8)


def backward_pass(closing, emission, usable, allowed_next):

    def frame_step(current, inputs):
        return (retreat(current, inputs[0], inputs[1], allowed_next), current)

    return lax.scan(frame_step, closing, (emission, usable), reverse=True, unroll=8)


def forward_final(initial, emission, usable, allowed):

    def frame_step(current, inputs):
        return (advance(current, inputs[0], inputs[1], allowed), None)

    return lax.scan(frame_step, initial, (emission, usable), unroll=8)[0]


def backward_final(closing, emission, usable, allowed_next):

    def frame_step(current, inputs):
        return (retreat(current, inputs[0], inputs[1], allowed_next), None)

    return lax.scan(frame_step, closing, (emission, usable), reverse=True, unroll=8)[0]


def gradients(logprob, forward_states, backward_states, usable, char_index):
    frames, utterances, states_wide = forward_states.shape
    summed = forward_states + backward_states
    highest = jnp.max(summed, axis=2, keepdims=True)
    log_total = highest + jnp.log(jnp.sum(jnp.exp(summed - highest), axis=2, keepdims=True))
    posterior = jnp.exp(summed - log_total) * usable[:, :, None].astype(jnp.float32)
    paired = posterior.reshape(frames, utterances, states_wide // 2, 2)
    blank_mass = jnp.sum(paired[:, :, :, 0], axis=2, keepdims=True)
    occupancy = jnp.concatenate([blank_mass, paired[:, :, :-1, 1]], axis=2)
    vocabulary = logprob.shape[2]
    one_hot = (
        char_index[:, :, None] == jnp.arange(vocabulary, dtype=jnp.int32)[None, None, :]
    ).astype(jnp.float32)
    char_mass = jnp.einsum("fup,upv->ufv", occupancy, one_hot, precision=lax.Precision.HIGHEST)
    keep = jnp.swapaxes(usable, 0, 1)[:, :, None].astype(jnp.float32)
    return ((jnp.exp(logprob) - char_mass) * keep).astype(jnp.bfloat16)


def shards(enc_rows, out_weight, labels, label_count, frame_count):
    utterances, frames, width_rows = enc_rows.shape
    vocabulary = out_weight.shape[1]
    flat_rows = enc_rows.reshape(utterances * frames, width_rows)
    logits = jnp.dot(flat_rows, out_weight, preferred_element_type=jnp.float32).reshape(
        utterances, frames, vocabulary
    )
    logprob = jax.nn.log_softmax(logits, axis=-1)
    emission, char_index = emissions(logprob, labels)
    allowed, allowed_next, initial, closing = lattice(labels, label_count)
    seq_index = lax.axis_index("seq")
    seq_count = lax.axis_size("seq")
    frame_index = seq_index * frames + jnp.arange(frames, dtype=jnp.int32)
    usable = frame_index[:, None] < frame_count[None, :]

    def run_forward(current):
        return forward_final(current, emission, usable, allowed)

    def run_backward(current):
        return backward_final(current, emission, usable, allowed_next)

    def keep_same(current):
        return current

    def both_turns(turn_index, carried):
        forward_in, backward_in = carried
        forward_out = lax.cond(seq_index == turn_index, run_forward, keep_same, forward_in)
        backward_out = lax.cond(
            seq_index == seq_count - 1 - turn_index, run_backward, keep_same, backward_in
        )
        forward_got = from_behind(forward_out, "seq", 1)
        backward_got = from_behind(backward_out, "seq", -1)
        forward_in = jnp.where(seq_index == turn_index + 1, forward_got, forward_in)
        backward_in = jnp.where(seq_index == seq_count - 2 - turn_index, backward_got, backward_in)
        return (forward_in, backward_in)

    forward_in, backward_in = lax.fori_loop(0, seq_count - 1, both_turns, (initial, closing))
    forward_states = forward_pass(forward_in, emission, usable, allowed)[1]
    backward_states = backward_pass(backward_in, emission, usable, allowed_next)[1]
    logit_grad = gradients(logprob, forward_states, backward_states, usable, char_index)
    flat_grad = logit_grad.reshape(utterances * frames, vocabulary)
    row_grad = lax.dot_general(
        flat_grad, out_weight, (((1,), (1,)), ((), ())), preferred_element_type=jnp.float32
    )
    row_grad = row_grad.astype(jnp.bfloat16).reshape(utterances, frames, width_rows)
    batch_total = utterances * lax.axis_size("dp")
    product = lax.dot_general(
        flat_rows, flat_grad, (((0,), (0,)), ((), ())), preferred_element_type=jnp.float32
    )
    partial_sum = lax.psum_scatter(product / batch_total, "dp", scatter_dimension=0, tiled=True)
    weight_grad = lax.psum_scatter(partial_sum, "seq", scatter_dimension=1, tiled=True)
    return (logit_grad, row_grad, weight_grad)


def solution(mesh):
    placed = (P("dp", "seq", None), P(), P("dp", None), P("dp"), P("dp"))
    return jax.shard_map(
        shards,
        mesh=mesh,
        in_specs=placed,
        out_specs=(P("dp", "seq", None), P("dp", "seq", None), P("dp", "seq")),
        check_vma=False,
    )
```

profile of v0, /device:TPU:0, one launch (start us, length us, event | category | flops | bytes accessed | tf_op | source)
XLA Modules:
  0.0 621.5 jit_solution(4673187423918094126)
XLA Ops:
  9.0 1.7 fusion.88
  11.1 161.0 %gather_fusion = f32[16384]{0:T(1024)S(1)} fusion(f32[4,64,512]{2,1,0:T(8,128)S(1)} %fusion.90, s32[16384]{0:T(1024)S(1)} %reshape.352), kind=kCustom, calls=%fused_computation | custom fusion | bytes 327680 | tf_op jit(solution)/shard_map/jit(take_along_axis)/gather | solution.py:72
  174.5 264.0 %while.76 = (s32[]{:T(128)}, f32[4,128]{1,0:T(4,128)S(1)}, f32[4,128]{1,0:T(4,128)S(1)}, s32[]{:T(128)}, f32[64,4,128]{2,1,0:T(4,128)}, /*index=5*/pred[4,128]{1...) while((s32[]{:T(128)}, f32[4,128]{1,0:T(4,128)S(1)}, ...), condition=%wide.region_11.12_spmd.clone, body=%wide.region_2.11_spmd.clone.sunk | while | flops 91421 | bytes 309747 | solution.py:172
  174.6 56.1 %conditional.6 = (f32[4,128]{1,0:T(4,128)}) conditional(s32[]{:T(128)} %convert_element_type.49, f32[4,128]{1,0:T(4,128)S(1)} %get-tuple-element.1156, (f32[64,4,128]{2,1,0:T(4,128)}, pred[64,4]{1,0:T(8,128)(4,1)S(1)}, pred[4,128]{1,0:T(4,128)(4,1)S(1)}, f32[4,128]{1,0:T(4,128)S(1)}) %tuple.249), branch_computations={%region_3.3_spmd, %region_4.6_spmd} | conditional | flops 45065 | bytes 90297 | solution.py:162
  175.2 55.5 %while.72 = (s32[]{:T(128)}, f32[4,128]{1,0:T(4,128)}, pred[8,8,4]{2,1,0:T(8,128)(4,1)S(1)}, pred[4,128]{1,0:T(4,128)(4,1)S(1)}, f32[8,8,4,128]{3,2,1,0:T(4,128)...) while((s32[]{:T(128)}, f32[4,128]{1,0:T(4,128)}, ...), condition=%wide.region_6.5_spmd, body=%wide.region_5.4_spmd.sunk | while | flops 45065 | bytes 86073 | solution.py:107
  180.8 1.4 fusion.167
  187.7 1.4 fusion.167
  194.7 1.4 fusion.167
  201.6 1.4 fusion.167
  208.5 1.4 fusion.167
  215.5 1.4 fusion.167
  222.4 1.4 fusion.167
  229.4 1.4 fusion.167
  232.6 1.3 collective-permute-start.1
  233.9 1.9 collective-permute-done.1
  236.5 57.6 %collective-permute-start = (f32[4,128]{1,0:T(4,128)}, f32[4,128]{1,0:T(4,128)S(1)}, u32[]{:S(2)}, u32[]{:S(2)}) collective-permute-start(f32[4,128]{1,0:T(4,128)} %get-tuple-element.1272), channel_id=1, source_target_pairs={{0,1},{1,2},{2,3},{4,5},{5,6},{6,7},{8,9},{9,10},{10,11},{12,13},{... | collective-permute-start | bytes 6152 | tf_op jit(solution)/shard_map/while/body/eval_jaxpr/ppermute | solution.py:12
  294.7 1.3 collective-permute-start.1
  296.0 1.9 collective-permute-done.1
  298.6 18.3 %collective-permute-start = (f32[4,128]{1,0:T(4,128)}, f32[4,128]{1,0:T(4,128)S(1)}, u32[]{:S(2)}, u32[]{:S(2)}) collective-permute-start(f32[4,128]{1,0:T(4,128)} %get-tuple-element.1272), channel_id=1, source_target_pairs={{0,1},{1,2},{2,3},{4,5},{5,6},{6,7},{8,9},{9,10},{10,11},{12,13},{... | collective-permute-start | bytes 6152 | tf_op jit(solution)/shard_map/while/body/eval_jaxpr/ppermute | solution.py:12
  317.5 1.3 collective-permute-start.1
  318.8 119.7 %collective-permute-done.1 = f32[4,128]{1,0:T(4,128)S(1)} collective-permute-done((f32[4,128]{1,0:T(4,128)}, f32[4,128]{1,0:T(4,128)S(1)}, u32[]{:S(2)}, u32[]{:S(2)}) %collective-permute-start.1) | collective-permute-done | bytes 2080 | tf_op jit(solution)/shard_map/while/body/eval_jaxpr/ppermute | solution.py:12
  438.6 15.2 %while.75 = (s32[]{:T(128)}, f32[4,128]{1,0:T(4,128)S(1)}, f32[8,8,4,128]{3,2,1,0:T(4,128)S(1)}, pred[8,8,4]{2,1,0:T(8,128)(4,1)S(1)}, f32[8,8,4,128]{3,2,1,0:T(...) while((s32[]{:T(128)}, f32[4,128]{1,0:T(4,128)S(1)}, ...), condition=%wide.region_15.16_spmd, body=%wide.region_14.15_spmd.sunk | while | flops 45065 | bytes 251225 | solution.py:99
  454.4 50.6 %while.74 = (s32[]{:T(128)}, f32[4,128]{1,0:T(4,128)S(1)}, f32[8,8,4,128]{3,2,1,0:T(4,128)S(1)}, pred[8,8,4]{2,1,0:T(8,128)(4,1)S(1)}, pred[4,128]{1,0:T(4,128)(...) while((s32[]{:T(128)}, f32[4,128]{1,0:T(4,128)S(1)}, ...), condition=%wide.region_13.14_spmd, body=%wide.region_12.13_spmd.sunk | while | flops 45064 | bytes 139129 | solution.py:91
  505.2 2.0 copy.50
  507.5 2.5 add.1033
  511.1 2.1 fusion.85
  513.2 3.2 copy.56
  516.5 73.2 %reduce-scatter.7.cloned.1.call-done = f32[160,512]{1,0:T(8,128)} async-done(((f32[1280,512]{1,0:T(8,128)}), f32[160,512]{1,0:T(8,128)}) %reduce-scatter.7.cloned.1.call-update) | async-done | bytes 327696
  589.7 2.0 copy.57
  591.7 1.4 convolution_convert_fusion
  593.1 19.9 %reduce-scatter.5.cloned.1.call-done = f32[160,128]{0,1:T(8,128)} async-done(((f32[160,512]{0,1:T(8,128)}), f32[160,128]{0,1:T(8,128)}) %reduce-scatter.5.cloned.1.call-update) | async-done | bytes 81936 | tf_op jit(solution)/shard_map/reduce_scatter | solution.py:186
  613.0 1.6 copy.54
  (533 shorter events, 124.5 us)
Async XLA Ops:
  7.2 1.8 copy-start
  7.2 582.5 %reduce-scatter.7.cloned.1.call-start = ((), (), s32[]{:S(2)}) async-start(), calls=%async_computation.3 | async-start | bytes 2949120
  172.2 2.0 copy-start.5
  172.2 2.1 copy-start.4
  230.7 3.2 collective-permute-start
  232.6 3.3 collective-permute-start.1
  236.5 59.5 %collective-permute-start = (f32[4,128]{1,0:T(4,128)}, f32[4,128]{1,0:T(4,128)S(1)}, u32[]{:S(2)}, u32[]{:S(2)}) collective-permute-start(f32[4,128]{1,0:T(4,128)} %get-tuple-element.1272), channel_id=1, source_target_pairs={{0,1},{1,2},{2,3},{4,5},{5,6},{6,7},{8,9},{9,10},{10,11},{12,13},{... | collective-permute-start | bytes 6152 | tf_op jit(solution)/shard_map/while/body/eval_jaxpr/ppermute | solution.py:12
  294.7 3.3 collective-permute-start.1
  298.6 20.2 %collective-permute-start = (f32[4,128]{1,0:T(4,128)}, f32[4,128]{1,0:T(4,128)S(1)}, u32[]{:S(2)}, u32[]{:S(2)}) collective-permute-start(f32[4,128]{1,0:T(4,128)} %get-tuple-element.1272), channel_id=1, source_target_pairs={{0,1},{1,2},{2,3},{4,5},{5,6},{6,7},{8,9},{9,10},{10,11},{12,13},{... | collective-permute-start | bytes 6152 | tf_op jit(solution)/shard_map/while/body/eval_jaxpr/ppermute | solution.py:12
  317.5 121.0 %collective-permute-start.1 = (f32[4,128]{1,0:T(4,128)}, f32[4,128]{1,0:T(4,128)S(1)}, u32[]{:S(2)}, u32[]{:S(2)}) collective-permute-start(f32[4,128]{1,0:T(4,128)} %get-tuple-element.1273), channel_id=1, source_target_pairs={{1,0},{2,1},{3,2},{5,4},{6,5},{7,6},{9,8},{10,9},{11,10},{13,12},{... | collective-permute-start | bytes 6152 | tf_op jit(solution)/shard_map/while/body/eval_jaxpr/ppermute | solution.py:12
  453.8 0.7 copy-start.2
  507.1 4.0 copy-start.3
  511.1 80.6 %copy-start.1 = (bf16[4,64,512]{2,1,0:T(8,128)(2,1)}, bf16[4,64,512]{2,1,0:T(8,128)(2,1)S(1)}, u32[]{:S(2)}) copy-start(bf16[4,64,512]{2,1,0:T(8,128)(2,1)S(1)} %fusion.92) | copy-start | bytes 786436
  516.5 96.6 %reduce-scatter.5.cloned.1.call-start = ((), (), s32[]{:S(2)}) async-start(), calls=%async_computation.2 | async-start | bytes 655360 | tf_op jit(solution)/shard_map/reduce_scatter | solution.py:186
Sparse Core Ops, SparseCore 0:
  516.6 73.0 reduce-scatter.6
  592.2 20.7 reduce-scatter.4
where the time goes:
time: 627 us; the launch traced here: 622 us
  waiting for transfers between devices  217 us (35%)
  local copies, waits for them, and re-layouts  189 us (30%)
  other arithmetic  114 us (18%)
  starting transfers between devices  81 us (13%)
  between operations  14.3 us (2%)
    gather x3, local copies, waits for them, and re-layouts, emissions(): jnp.take_along_axis(logprob, jnp.broadcast_to(char_index[:, None, :], (ut...  161 us
    ppermute x6, waiting for transfers between devices, from_behind(): return lax.ppermute(block, axis, route)  124 us
    ppermute x6, starting transfers between devices, from_behind(): return lax.ppermute(block, axis, route)  80.9 us
    unnamed x3, waiting for transfers between devices  73.2 us
    select_n x64, other arithmetic, advance(): return jnp.where(usable[:, None], fresh, current)  55.3 us
    while x64, other arithmetic  44.4 us
    reduce_scatter x1, waiting for transfers between devices, shards(): lax.psum_scatter(partial_sum, 'seq', scatter_dimension=1, tiled=True)  19.9 us
  transfers between devices with their start and end apart: 8, of which 5 were waited for; matrix products, arithmetic and copies ran while one was open for 1% of the time, Pallas kernels for 0%

commit v1 on v0

v1 whole, which is shorter than its diff:
```python
import functools

import jax
import jax.numpy as jnp
from jax import lax
from jax.experimental import pallas as pl
from jax.experimental.pallas import tpu as pltpu
from jax.sharding import PartitionSpec as P

negative_fill = -1e30
LANES = 128
SPLIT = 2
UNROLL = 16
MESH = pl.DeviceIdType.MESH
BOTH_LAST = (((1,), (1,)), ((), ()))


def three_parts(values):
    high = values.astype(jnp.bfloat16)
    rest = values - high.astype(jnp.float32)
    middle = rest.astype(jnp.bfloat16)
    low = (rest - middle.astype(jnp.float32)).astype(jnp.bfloat16)
    return high, middle, low


def emission_kernel(seq_count, utterances, enc_ref, weight_ref, chars_ref,
                    logprob_ref, gathered_ref, send_sems, recv_sems):
    me = lax.axis_index("seq")
    barrier = pltpu.get_barrier_semaphore()
    for step in range(1, seq_count):
        peer = lax.rem(me + step, seq_count)
        pl.semaphore_signal(barrier, inc=1, device_id={"seq": peer}, device_id_type=MESH)
    frames = enc_ref.shape[0] // utterances
    vocabulary = weight_ref.shape[1]
    groups = gathered_ref.shape[1]
    pack = utterances // groups
    logits = jnp.dot(enc_ref[...], weight_ref[...], preferred_element_type=jnp.float32)
    highest = jnp.max(logits, axis=1, keepdims=True)
    total = jnp.sum(jnp.exp(logits - highest), axis=1, keepdims=True)
    logprob = logits - (highest + jnp.log(total))
    rows = lax.broadcasted_iota(jnp.int32, (vocabulary, LANES), 0)
    for group in range(groups):
        picked = jnp.zeros((frames, LANES), jnp.float32)
        for inner in range(pack):
            utterance = group * pack + inner
            one_hot = jnp.where(
                rows == chars_ref[pl.ds(utterance, 1), :], 1.0, 0.0
            ).astype(jnp.bfloat16)
            mine = logprob[utterance * frames:(utterance + 1) * frames]
            for part in three_parts(mine):
                picked += jnp.dot(part, one_hot, preferred_element_type=jnp.float32)
        gathered_ref[me, group] = picked
    logprob_ref[...] = logprob
    pl.semaphore_wait(barrier, seq_count - 1)
    copies = []
    for step in range(1, seq_count):
        peer = lax.rem(me + step, seq_count)
        copy = pltpu.make_async_remote_copy(
            src_ref=gathered_ref.at[me],
            dst_ref=gathered_ref.at[me],
            send_sem=send_sems.at[step - 1],
            recv_sem=recv_sems.at[step - 1],
            device_id={"seq": peer},
            device_id_type=MESH,
        )
        copy.start()
        copies.append(copy)
    for copy in copies:
        copy.wait()


def take_lanes(values, index):
    return jnp.take_along_axis(values, index, axis=1)


def lattice_kernel(length, utterances, place_ref, gathered_ref, meta_ref, logprob_ref, enc_ref,
                   weight_ref, logit_ref, row_ref, term_ref, level_ref, factor_ref, mass_ref):
    seq_count, groups, frames = gathered_ref.shape[:3]
    steps = seq_count * frames
    rows = 2 * utterances
    slots = length + 1
    pack = utterances // groups
    span = LANES * SPLIT
    shape = (rows, LANES)
    row = lax.broadcasted_iota(jnp.int32, shape, 0)
    lane = lax.broadcasted_iota(jnp.int32, shape, 1)
    forward = row < utterances
    utterance = lax.rem(row, utterances)
    offset = lax.rem(utterance, pack) * slots
    label_rows = meta_ref[0]
    label_count = meta_ref[1]
    frame_count = meta_ref[2]
    first_usable = jnp.where(forward, 0, steps - frame_count)

    label_index, label_fill, jump_fill, label_start = [], [], [], []
    blank_fill, blank_start, label_chars = [], [], []
    for r in range(SPLIT):
        place = lane * SPLIT + r
        j = jnp.where(forward, place, span - 1 - place)
        real = j < length
        label_index.append(offset + jnp.clip(j, 0, slots - 1))
        label_fill.append(jnp.where(real, 0.0, negative_fill))
        before = jnp.where(forward, j - 1, j + 1)
        here_char = take_lanes(label_rows, jnp.clip(j, 0, LANES - 1))
        before_char = take_lanes(label_rows, jnp.clip(before, 0, LANES - 1))
        can_jump = real & (before >= 0) & (before < length) & (here_char != before_char)
        jump_fill.append(jnp.where(can_jump, 0.0, negative_fill))
        label_chars.append(jnp.where(real, here_char, -1))
        label_begin = j == jnp.where(forward, 0, label_count - 1)
        label_start.append(jnp.where(label_begin, 0.0, negative_fill))
        blank = jnp.where(forward, j, lax.rem(j + 1, span))
        blank_fill.append(jnp.where(blank < slots, 0.0, negative_fill))
        blank_begin = blank == jnp.where(forward, 0, label_count)
        blank_start.append(jnp.where(blank_begin, 0.0, negative_fill))
    blank_index = offset + slots - 1
    row_group = utterance // pack

    def frame_row(group, step):
        block = step // frames
        inside = lax.rem(step, frames)
        return jnp.broadcast_to(gathered_ref[block, group, pl.ds(inside, 1), :], shape)

    def raw_emission(step):
        raw = None
        for group in range(groups):
            early = frame_row(group, step)
            late = frame_row(group, steps - 1 - step)
            both = jnp.where(forward, early, late)
            raw = both if raw is None else jnp.where(row_group == group, both, raw)
        return raw

    def one_step(step, state):
        labels_v, blanks_v, labels_x, blanks_x = state
        raw = raw_emission(step)
        blank_emission = take_lanes(raw, blank_index)
        usable = step >= first_usable
        next_labels_v, next_blanks_v, next_labels_x, next_blanks_x = [], [], [], []
        full_labels, full_blanks = [], []
        for r in range(SPLIT):
            full_labels.append(labels_v[r] + (take_lanes(raw, label_index[r]) + label_fill[r]))
            full_blanks.append(blanks_v[r] + (blank_emission + blank_fill[r]))
            level_ref[step, r] = jnp.where(forward, full_labels[r], labels_v[r])
            level_ref[step, SPLIT + r] = jnp.where(forward, full_blanks[r], blanks_v[r])
            factor_ref[step, r] = labels_x[r]
            factor_ref[step, SPLIT + r] = blanks_x[r]
        for r in range(SPLIT):
            if r == 0:
                behind_v = pltpu.roll(full_labels[SPLIT - 1], 1, 1)
                behind_x = pltpu.roll(labels_x[SPLIT - 1], 1, 1)
            else:
                behind_v = full_labels[r - 1]
                behind_x = labels_x[r - 1]
            jump_v = behind_v + jump_fill[r]
            pivot = jnp.maximum(jnp.maximum(full_blanks[r], jump_v), full_labels[r])
            fresh_x = (
                jnp.exp(full_labels[r] - pivot) * labels_x[r]
                + jnp.exp(full_blanks[r] - pivot) * blanks_x[r]
                + jnp.exp(jump_v - pivot) * behind_x
            )
            next_labels_v.append(jnp.where(usable, pivot, label_start[r]))
            next_labels_x.append(jnp.where(usable, fresh_x, 1.0))
            pivot = jnp.maximum(full_blanks[r], behind_v)
            fresh_x = (
                jnp.exp(full_blanks[r] - pivot) * blanks_x[r]
                + jnp.exp(behind_v - pivot) * behind_x
            )
            next_blanks_v.append(jnp.where(usable, pivot, blank_start[r]))
            next_blanks_x.append(jnp.where(usable, fresh_x, 1.0))
        return (tuple(next_labels_v), tuple(next_blanks_v), tuple(next_labels_x), tuple(next_blanks_x))

    ones = (jnp.ones(shape, jnp.float32),) * SPLIT

    def run_block(block, state):
        labels_v, blanks_v = state
        full = (labels_v, blanks_v, ones, ones)
        for inner in range(UNROLL):
            full = one_step(block * UNROLL + inner, full)
        labels_v, blanks_v, labels_x, blanks_x = full
        labels_v = tuple(v + jnp.log(x) for v, x in zip(labels_v, labels_x))
        blanks_v = tuple(v + jnp.log(x) for v, x in zip(blanks_v, blanks_x))
        return labels_v, blanks_v

    lax.fori_loop(0, steps // UNROLL, run_block, (tuple(label_start), tuple(blank_start)))

    start = place_ref[0] * frames
    reverse = LANES - 1 - lane
    reverse_next = lax.rem(LANES - lane, LANES)
    chunk = 8

    def posterior_block(block, carry):
        for inner in range(chunk):
            frame = block * chunk + inner
            ahead = start + frame
            back = steps - 1 - ahead
            summed = []
            for r in range(SPLIT):
                other = SPLIT - 1 - r
                turned = take_lanes(level_ref[back, other] + jnp.log(factor_ref[back, other]), reverse)
                summed.append(
                    level_ref[ahead, r] + jnp.log(factor_ref[ahead, r])
                    + pltpu.roll(turned, utterances, 0)
                )
            for r in range(SPLIT):
                other = SPLIT + (SPLIT - r) % SPLIT
                turned = take_lanes(
                    level_ref[back, other] + jnp.log(factor_ref[back, other]),
                    reverse_next if r == 0 else reverse,
                )
                summed.append(
                    level_ref[ahead, SPLIT + r] + jnp.log(factor_ref[ahead, SPLIT + r])
                    + pltpu.roll(turned, utterances, 0)
                )
            highest = functools.reduce(jnp.maximum, summed)
            highest = jnp.max(highest, axis=1, keepdims=True)
            powers = [jnp.exp(term - highest) for term in summed]
            total = jnp.sum(sum(powers), axis=1, keepdims=True)
            scale = jnp.where(ahead < frame_count, 1.0, 0.0) / total
            for r in range(SPLIT):
                mass_ref[r, frame] = powers[r] * scale
            mass_ref[SPLIT, frame] = sum(powers[SPLIT:]) * scale
        return carry

    lax.fori_loop(0, frames // chunk, posterior_block, 0)

    vocabulary = logprob_ref.shape[1]
    chars = lax.broadcasted_iota(jnp.int32, (vocabulary, LANES), 0)
    columns = lax.broadcasted_iota(jnp.int32, (frames, vocabulary), 1)
    times = start + lax.broadcasted_iota(jnp.int32, (frames, vocabulary), 0)
    for u in range(utterances):
        mass = jnp.zeros((frames, vocabulary), jnp.float32)
        for r in range(SPLIT):
            one_hot = jnp.where(chars == label_chars[r][u:u + 1, :], 1.0, 0.0).astype(jnp.bfloat16)
            for part in three_parts(mass_ref[r, :, u, :])[:2]:
                mass += lax.dot_general(part, one_hot, BOTH_LAST, preferred_element_type=jnp.float32)
        blank_mass = jnp.sum(mass_ref[SPLIT, :, u, :], axis=1, keepdims=True)
        mass += jnp.where(columns == 0, blank_mass, 0.0)
        own = slice(u * frames, (u + 1) * frames)
        count = jnp.broadcast_to(frame_count[u:u + 1, :1], (frames, vocabulary))
        kept = jnp.where(times < count, jnp.exp(logprob_ref[own, :]) - mass, 0.0)
        logit_ref[own, :] = kept.astype(jnp.bfloat16)
    grad = logit_ref[...]
    row_ref[...] = lax.dot_general(
        grad, weight_ref[...], BOTH_LAST, preferred_element_type=jnp.float32
    ).astype(jnp.bfloat16)
    term_ref[...] = lax.dot_general(
        enc_ref[...], grad, (((0,), (0,)), ((), ())), preferred_element_type=jnp.float32
    )


def shards(enc_rows, out_weight, labels, label_count, frame_count):
    utterances, frames, width = enc_rows.shape
    vocabulary = out_weight.shape[1]
    length = labels.shape[1]
    slots = length + 1
    pack = LANES // slots
    groups = utterances // pack
    seq_count = lax.axis_size("seq")
    flat_rows = enc_rows.reshape(utterances * frames, width)
    vmem = pl.BlockSpec(memory_space=pltpu.VMEM)

    own_chars = jnp.concatenate([labels, jnp.zeros((utterances, 1), jnp.int32)], axis=1)
    segment = jnp.arange(LANES, dtype=jnp.int32)[None, :] // slots
    own_segment = jnp.arange(utterances, dtype=jnp.int32)[:, None] % pack
    chars = jnp.where(segment == own_segment, jnp.tile(own_chars, (1, pack)), -1)
    logprob, gathered = pl.pallas_call(
        functools.partial(emission_kernel, seq_count, utterances),
        out_shape=(
            jax.ShapeDtypeStruct((utterances * frames, vocabulary), jnp.float32),
            jax.ShapeDtypeStruct((seq_count, groups, frames, LANES), jnp.float32),
        ),
        in_specs=[vmem] * 3,
        out_specs=(vmem, vmem),
        scratch_shapes=[
            pltpu.SemaphoreType.DMA((seq_count - 1,)),
            pltpu.SemaphoreType.DMA((seq_count - 1,)),
        ],
        compiler_params=pltpu.CompilerParams(collective_id=0, has_side_effects=True),
        name="emission",
    )(flat_rows, out_weight, chars)

    rows = 2 * utterances
    padded = jnp.pad(labels, ((0, 0), (0, LANES - length)))
    meta = jnp.stack(
        [
            padded,
            jnp.broadcast_to(label_count[:, None], (utterances, LANES)),
            jnp.broadcast_to(frame_count[:, None], (utterances, LANES)),
        ]
    )
    meta = jnp.concatenate([meta, meta], axis=1)
    steps = seq_count * frames
    logit_grad, row_grad, term = pl.pallas_call(
        functools.partial(lattice_kernel, length, utterances),
        out_shape=(
            jax.ShapeDtypeStruct((utterances * frames, vocabulary), jnp.bfloat16),
            jax.ShapeDtypeStruct((utterances * frames, width), jnp.bfloat16),
            jax.ShapeDtypeStruct((width, vocabulary), jnp.float32),
        ),
        in_specs=[pl.BlockSpec(memory_space=pltpu.SMEM)] + [vmem] * 5,
        out_specs=(vmem, vmem, vmem),
        scratch_shapes=[
            pltpu.VMEM((steps, 2 * SPLIT, rows, LANES), jnp.float32),
            pltpu.VMEM((steps, 2 * SPLIT, rows, LANES), jnp.float32),
            pltpu.VMEM((SPLIT + 1, frames, rows, LANES), jnp.float32),
        ],
        compiler_params=pltpu.CompilerParams(vmem_limit_bytes=60 * 1024 * 1024),
        name="lattice",
    )(lax.axis_index("seq").reshape(1), gathered, meta, logprob, flat_rows, out_weight)
    batch_total = utterances * lax.axis_size("dp")
    partial_sum = lax.psum_scatter(term / batch_total, "dp", scatter_dimension=0, tiled=True)
    weight_grad = lax.psum_scatter(partial_sum, "seq", scatter_dimension=1, tiled=True)
    return (
        logit_grad.reshape(utterances, frames, vocabulary),
        row_grad.reshape(utterances, frames, width),
        weight_grad,
    )


def solution(mesh):
    placed = (P("dp", "seq", None), P(), P("dp", None), P("dp"), P("dp"))
    return jax.shard_map(
        shards,
        mesh=mesh,
        in_specs=placed,
        out_specs=(P("dp", "seq", None), P("dp", "seq", None), P("dp", "seq")),
        check_vma=False,
    )
```

time: 627 us -> 147 us (0.23)
  local copies, waits for them, and re-layouts: 189 us -> 2.91 us
  waiting for transfers between devices: 217 us -> 94.7 us
  other arithmetic: 114 us -> 4.81 us
  starting transfers between devices: 81 us -> 0.08 us
  Pallas kernels: 0 us -> 30 us
    gather x3 -> x0, local copies, waits for them, and re-layouts: 161 us -> none  [emissions(): jnp.take_along_axis(logprob, jnp.broadcast_to(char_index[:, None, :], (ut...]
    ppermute x6 -> x0, waiting for transfers between devices: 124 us -> none  [from_behind(): return lax.ppermute(block, axis, route)]
    ppermute x6 -> x0, starting transfers between devices: 80.9 us -> none  [from_behind(): return lax.ppermute(block, axis, route)]
    unnamed x3 -> x2, waiting for transfers between devices: 73.2 us -> 0.03 us
    reduce_scatter x0 -> x1, waiting for transfers between devices: none -> 72.1 us  [shards(): lax.psum_scatter(term / batch_total, 'dp', scatter_dimension=0, tiled=True)]
    select_n x81 -> x3, other arithmetic: 56 us -> 0.65 us  [the longest x1 0.65 us: shards(): jnp.where(segment == own_segment, jnp.tile(own_chars, (1, pack)), -1)]
    while x64 -> x0, other arithmetic: 44.4 us -> none
    pallas_call x0 -> x2, Pallas kernels: none -> 30 us  [the longest x1 20.6 us: shards(): pl.pallas_call(functools.partial(lattice_kernel, length, utterances), out...]
  transfers between devices with their start and end apart: 8 -> 2, of which waited for: 5 -> 2; matrix products, arithmetic and copies ran while one was open for 1% -> 0% of each run, Pallas kernels for 0% -> 0%
where the time goes in v1:
time: 147 us
  waiting for transfers between devices  94.7 us (64%)
  Pallas kernels  30 us (20%)
  between operations  14.1 us (10%)
  other arithmetic  4.81 us (3%)
  local copies, waits for them, and re-layouts  2.91 us (2%)
    reduce_scatter x1, waiting for transfers between devices, shards(): lax.psum_scatter(term / batch_total, 'dp', scatter_dimension=0, tiled=True)  72.1 us
    reduce_scatter x1, waiting for transfers between devices, shards(): lax.psum_scatter(partial_sum, 'seq', scatter_dimension=1, tiled=True)  22.6 us
    pallas_call x1, Pallas kernels, shards(): pl.pallas_call(functools.partial(lattice_kernel, length, utterances), out...  20.6 us
    pallas_call x1, Pallas kernels, shards(): pl.pallas_call(functools.partial(emission_kernel, seq_count, utterances),...  9.37 us
    div x1, other arithmetic, shards(): term / batch_total  3.55 us
  transfers between devices with their start and end apart: 2, of which 2 were waited for; matrix products, arithmetic and copies ran while one was open for 0% of the time, Pallas kernels for 0%

profile of v1, /device:TPU:0, one launch (start us, length us, event | category | flops | bytes accessed | tf_op | source)
XLA Modules:
  0.0 146.6 jit_solution(17947900325423321305)
XLA Ops:
  7.2 0.0 reduce-scatter.3.cloned.1.call-start
  7.2 0.7 pad_bitcast_fusion
  7.9 0.7 concatenate.6
  8.6 0.1 tile.10
  8.7 0.6 compare_select_fusion.chars_ref
  9.3 0.7 stack_broadcast_in_dim.4
  10.1 0.7 stack_broadcast_in_dim.5
  10.8 0.6 add_add_fusion.meta_ref
  11.4 9.4 %emission.1 = (f32[256,512]{1,0:T(8,128)}, f32[4,2,64,128]{3,2,1,0:T(8,128)}) custom-call(bf16[256,1280]{1,0:T(8,128)(2,1)} %bitcast.6, bf16[1280,512]{1,0:T(8,128)(2,1)} %weight_ref.3, s32[4,128]{1,0:T(4,128)} %compare_select_fusion.chars_ref), custom_call_target="tpu_custom_call" | custom-call | tf_op jit(solution)/shard_map/emission/pallas_call | solution.py:265
  20.8 20.6 %lattice.1 = (bf16[256,512]{1,0:T(8,128)(2,1)}, bf16[256,1280]{1,0:T(8,128)(2,1)}, f32[1280,512]{1,0:T(8,128)}) custom-call(s32[1]{0:T(128)} %bitcast.place_ref, f32[4,2,64,128]{3,2,1,0:T(8,128)} %get-tuple-element.8.gathered_ref, s32[3,8,128]{2,1,0:T(8,128)} %add_add_fusion.meta_ref, f32[256,512]{1,0:T(8,128)} %get-tuple-element.9.logprob_ref, ...), custom_call_target="tpu_custom_call" | custom-call | tf_op jit(solution)/shard_map/lattice/pallas_call | solution.py:292
  41.4 3.6 %broadcast_multiply_fusion = f32[1280,512]{1,0:T(8,128)} fusion(f32[1280,512]{1,0:T(8,128)} %get-tuple-element.12), kind=kLoop, calls=%fused_computation | loop fusion | flops 655360 | bytes 5242880 | tf_op jit(solution)/shard_map/div | solution.py:310
  44.9 0.0 reduce-scatter.3.cloned.1.call-update
  45.0 0.0 reduce-scatter.5.cloned.1.call-start
  45.0 72.1 %reduce-scatter.3.cloned.1.call-done = f32[160,512]{1,0:T(8,128)} async-done(((f32[1280,512]{1,0:T(8,128)}), f32[160,512]{1,0:T(8,128)}) %reduce-scatter.3.cloned.1.call-update) | async-done | bytes 327696 | tf_op jit(solution)/shard_map/reduce_scatter | solution.py:310
  117.1 0.0 reduce-scatter.5.cloned.1.call-update
  117.1 22.6 %reduce-scatter.5.cloned.1.call-done = f32[160,128]{1,0:T(8,128)} async-done(((f32[160,512]{1,0:T(8,128)}), f32[160,128]{1,0:T(8,128)}) %reduce-scatter.5.cloned.1.call-update) | async-done | bytes 81936 | tf_op jit(solution)/shard_map/reduce_scatter | solution.py:311
  (3 shorter events, 0.0 us)
Async XLA Ops:
  7.2 109.9 %reduce-scatter.3.cloned.1.call-start = ((), (), s32[]{:S(2)}) async-start(), calls=%async_computation.2 | async-start | bytes 2949120 | tf_op jit(solution)/shard_map/reduce_scatter | solution.py:310
  45.0 94.8 %reduce-scatter.5.cloned.1.call-start = ((), (), s32[]{:S(2)}) async-start(), calls=%async_computation.3 | async-start | bytes 409600 | tf_op jit(solution)/shard_map/reduce_scatter | solution.py:311
Sparse Core Ops, SparseCore 0:
  45.1 71.9 reduce-scatter.2
  120.1 19.5 reduce-scatter.4

commit v2 on v1

--- a/solution.py
+++ b/solution.py
@@ -23,8 +23,17 @@
     return high, middle, low
 
 
-def emission_kernel(seq_count, utterances, enc_ref, weight_ref, chars_ref,
-                    logprob_ref, gathered_ref, send_sems, recv_sems):
+def label_table(labels_ref, table_ref):
+    utterances, length = labels_ref.shape
+    table_ref[...] = jnp.zeros_like(table_ref)
+    table_ref[0:utterances, 0:length] = labels_ref[...]
+    table_ref[utterances:2 * utterances, 0:length] = labels_ref[...]
+    return table_ref[...]
+
+
+def emission_kernel(seq_count, enc_ref, weight_ref, labels_ref,
+                    logprob_ref, gathered_ref, table_ref, send_sems, recv_sems):
+    utterances, length = labels_ref.shape
     me = lax.axis_index("seq")
     barrier = pltpu.get_barrier_semaphore()
     for step in range(1, seq_count):
@@ -39,12 +48,18 @@
     total = jnp.sum(jnp.exp(logits - highest), axis=1, keepdims=True)
     logprob = logits - (highest + jnp.log(total))
     rows = lax.broadcasted_iota(jnp.int32, (vocabulary, LANES), 0)
+    table = label_table(labels_ref, table_ref)
+    lane = lax.broadcasted_iota(jnp.int32, table.shape, 1)
     for group in range(groups):
         picked = jnp.zeros((frames, LANES), jnp.float32)
         for inner in range(pack):
             utterance = group * pack + inner
+            begin = inner * (length + 1)
+            placed = pltpu.roll(table, begin, 1) if begin else table
+            inside = (lane >= begin) & (lane <= begin + length)
+            placed = jnp.where(inside, placed, -1)
             one_hot = jnp.where(
-                rows == chars_ref[pl.ds(utterance, 1), :], 1.0, 0.0
+                rows == placed[utterance:utterance + 1, :], 1.0, 0.0
             ).astype(jnp.bfloat16)
             mine = logprob[utterance * frames:(utterance + 1) * frames]
             for part in three_parts(mine):
@@ -73,8 +88,17 @@
     return jnp.take_along_axis(values, index, axis=1)
 
 
-def lattice_kernel(length, utterances, place_ref, gathered_ref, meta_ref, logprob_ref, enc_ref,
-                   weight_ref, logit_ref, row_ref, term_ref, level_ref, factor_ref, mass_ref):
+def spread(count_ref, utterance):
+    values = jnp.full(utterance.shape, count_ref[0], jnp.int32)
+    for u in range(1, count_ref.shape[0]):
+        values = jnp.where(utterance == u, count_ref[u], values)
+    return values
+
+
+def lattice_kernel(label_count_ref, frame_count_ref, gathered_ref, labels_ref, logprob_ref, enc_ref,
+                   weight_ref, logit_ref, row_ref, term_ref, table_ref, level_ref, factor_ref,
+                   mass_ref):
+    utterances, length = labels_ref.shape
     seq_count, groups, frames = gathered_ref.shape[:3]
     steps = seq_count * frames
     rows = 2 * utterances
@@ -87,9 +111,9 @@
     forward = row < utterances
     utterance = lax.rem(row, utterances)
     offset = lax.rem(utterance, pack) * slots
-    label_rows = meta_ref[0]
-    label_count = meta_ref[1]
-    frame_count = meta_ref[2]
+    label_rows = label_table(labels_ref, table_ref)
+    label_count = spread(label_count_ref, utterance)
+    frame_count = spread(frame_count_ref, utterance)
     first_usable = jnp.where(forward, 0, steps - frame_count)
 
     label_index, label_fill, jump_fill, label_start = [], [], [], []
@@ -182,7 +206,7 @@
 
     lax.fori_loop(0, steps // UNROLL, run_block, (tuple(label_start), tuple(blank_start)))
 
-    start = place_ref[0] * frames
+    start = lax.axis_index("seq") * frames
     reverse = LANES - 1 - lane
     reverse_next = lax.rem(LANES - lane, LANES)
     chunk = 8
@@ -235,16 +259,118 @@
         blank_mass = jnp.sum(mass_ref[SPLIT, :, u, :], axis=1, keepdims=True)
         mass += jnp.where(columns == 0, blank_mass, 0.0)
         own = slice(u * frames, (u + 1) * frames)
-        count = jnp.broadcast_to(frame_count[u:u + 1, :1], (frames, vocabulary))
-        kept = jnp.where(times < count, jnp.exp(logprob_ref[own, :]) - mass, 0.0)
+        kept = jnp.where(times < frame_count_ref[u], jnp.exp(logprob_ref[own, :]) - mass, 0.0)
         logit_ref[own, :] = kept.astype(jnp.bfloat16)
     grad = logit_ref[...]
     row_ref[...] = lax.dot_general(
         grad, weight_ref[...], BOTH_LAST, preferred_element_type=jnp.float32
     ).astype(jnp.bfloat16)
-    term_ref[...] = lax.dot_general(
-        enc_ref[...], grad, (((0,), (0,)), ((), ())), preferred_element_type=jnp.float32
-    )
+    seq_blocks, dp_blocks, block_rows, block_columns = term_ref.shape
+    for s in range(seq_blocks):
+        term_ref[s] = lax.dot_general(
+            enc_ref[...], grad[:, s * block_columns:(s + 1) * block_columns],
+            (((0,), (0,)), ((), ())), preferred_element_type=jnp.float32,
+        ).reshape(dp_blocks, block_rows, block_columns)
+
+
+def binary_digits(axis, count):
+    index = lax.axis_index(axis)
+    digits = []
+    step = 1
+    while step < count:
+        digit = lax.rem(index // step, 2)
+        digits.append((axis, digit, index + step * (1 - 2 * digit)))
+        step *= 2
+    return digits
+
+
+def halving_plan(seq_count, dp_count):
+    seq_bits = [("seq", i) for i in range(seq_count.bit_length() - 1)]
+    dp_bits = [("dp", i) for i in range(dp_count.bit_length() - 1)]
+    first, others = seq_bits[:1], seq_bits[1:]
+    along = first + others + dp_bits
+    across = first + dp_bits[:1] + others + dp_bits[1:]
+    held = seq_bits[::-1] + dp_bits[::-1]
+    return held, (along, across)
+
+
+def row_chunks(rows):
+    quarter = -(-rows // 4 // 8) * 8
+    return [(low, min(quarter, rows - low)) for low in range(0, rows, quarter)]
+
+
+def reduce_kernel(seq_count, dp_count, batch_total, term_ref, out_ref, *scratch):
+    digits = {
+        (axis, i): entry
+        for axis, count in (("seq", seq_count), ("dp", dp_count))
+        for i, entry in enumerate(binary_digits(axis, count))
+    }
+    barrier = pltpu.get_barrier_semaphore()
+    for axis, digit, partner in digits.values():
+        pl.semaphore_signal(barrier, inc=1, device_id={axis: partner}, device_id_type=MESH)
+    pl.semaphore_wait(barrier, len(digits))
+    held, orders = halving_plan(seq_count, dp_count)
+    chunks = row_chunks(term_ref.shape[-2])
+    stages = len(held)
+    send_sems, recv_sems = scratch[-2:]
+    landing = [scratch[c * stages:(c + 1) * stages] for c in range(len(chunks))]
+    current = [term_ref.at[(slice(None),) * stages + (pl.ds(low, size),)] for low, size in chunks]
+    names = [list(held) for _ in chunks]
+    pending = [None] * len(chunks)
+
+    def finish(c, stage):
+        copy, kept = pending[c]
+        copy.wait()
+        target = landing[c][stage]
+        target[...] += kept[...]
+        current[c] = target
+
+    for stage in range(stages):
+        for c in range(len(chunks)):
+            if stage:
+                finish(c, stage - 1)
+            bit = orders[c % 2][stage]
+            position = names[c].index(bit)
+            names[c].remove(bit)
+            axis, digit, partner = digits[bit]
+            ahead = (slice(None),) * position
+            copy = pltpu.make_async_remote_copy(
+                src_ref=current[c].at[ahead + (1 - digit,)],
+                dst_ref=landing[c][stage],
+                send_sem=send_sems.at[c, stage],
+                recv_sem=recv_sems.at[c, stage],
+                device_id={axis: partner},
+                device_id_type=MESH,
+            )
+            copy.start()
+            pending[c] = (copy, current[c].at[ahead + (digit,)])
+    for c, (low, size) in enumerate(chunks):
+        copy, kept = pending[c]
+        copy.wait()
+        out_ref[low:low + size] = (landing[c][stages - 1][...] + kept[...]) / batch_total
+
+
+def reduce_terms(term, batch_total):
+    seq_count, dp_count, rows, columns = term.shape
+    held, orders = halving_plan(seq_count, dp_count)
+    stages = len(held)
+    chunks = row_chunks(rows)
+    scratch = []
+    for low, size in chunks:
+        for stage in range(stages):
+            scratch.append(pltpu.VMEM((2,) * (stages - 1 - stage) + (size, columns), jnp.float32))
+    vmem = pl.BlockSpec(memory_space=pltpu.VMEM)
+    return pl.pallas_call(
+        functools.partial(reduce_kernel, seq_count, dp_count, batch_total),
+        out_shape=jax.ShapeDtypeStruct((rows, columns), jnp.float32),
+        in_specs=[vmem],
+        out_specs=vmem,
+        scratch_shapes=scratch + [pltpu.SemaphoreType.DMA((len(chunks), stages))] * 2,
+        compiler_params=pltpu.CompilerParams(
+            collective_id=1, has_side_effects=True, vmem_limit_bytes=40 * 1024 * 1024
+        ),
+        name="reduce",
+    )(term.reshape((2,) * stages + (rows, columns)))
 
 
 def shards(enc_rows, out_weight, labels, label_count, frame_count):
@@ -258,12 +384,8 @@
     flat_rows = enc_rows.reshape(utterances * frames, width)
     vmem = pl.BlockSpec(memory_space=pltpu.VMEM)
 
-    own_chars = jnp.concatenate([labels, jnp.zeros((utterances, 1), jnp.int32)], axis=1)
-    segment = jnp.arange(LANES, dtype=jnp.int32)[None, :] // slots
-    own_segment = jnp.arange(utterances, dtype=jnp.int32)[:, None] % pack
-    chars = jnp.where(segment == own_segment, jnp.tile(own_chars, (1, pack)), -1)
     logprob, gathered = pl.pallas_call(
-        functools.partial(emission_kernel, seq_count, utterances),
+        functools.partial(emission_kernel, seq_count),
         out_shape=(
             jax.ShapeDtypeStruct((utterances * frames, vocabulary), jnp.float32),
             jax.ShapeDtypeStruct((seq_count, groups, frames, LANES), jnp.float32),
@@ -271,44 +393,39 @@
         in_specs=[vmem] * 3,
         out_specs=(vmem, vmem),
         scratch_shapes=[
+            pltpu.VMEM((2 * utterances, LANES), jnp.int32),
             pltpu.SemaphoreType.DMA((seq_count - 1,)),
             pltpu.SemaphoreType.DMA((seq_count - 1,)),
         ],
         compiler_params=pltpu.CompilerParams(collective_id=0, has_side_effects=True),
         name="emission",
-    )(flat_rows, out_weight, chars)
+    )(flat_rows, out_weight, labels)
 
     rows = 2 * utterances
-    padded = jnp.pad(labels, ((0, 0), (0, LANES - length)))
-    meta = jnp.stack(
-        [
-            padded,
-            jnp.broadcast_to(label_count[:, None], (utterances, LANES)),
-            jnp.broadcast_to(frame_count[:, None], (utterances, LANES)),
-        ]
-    )
-    meta = jnp.concatenate([meta, meta], axis=1)
     steps = seq_count * frames
+    dp_count = lax.axis_size("dp")
+    smem = pl.BlockSpec(memory_space=pltpu.SMEM)
     logit_grad, row_grad, term = pl.pallas_call(
-        functools.partial(lattice_kernel, length, utterances),
+        lattice_kernel,
         out_shape=(
             jax.ShapeDtypeStruct((utterances * frames, vocabulary), jnp.bfloat16),
             jax.ShapeDtypeStruct((utterances * frames, width), jnp.bfloat16),
-            jax.ShapeDtypeStruct((width, vocabulary), jnp.float32),
+            jax.ShapeDtypeStruct(
+                (seq_count, dp_count, width // dp_count, vocabulary // seq_count), jnp.float32
+            ),
         ),
-        in_specs=[pl.BlockSpec(memory_space=pltpu.SMEM)] + [vmem] * 5,
+        in_specs=[smem, smem] + [vmem] * 5,
         out_specs=(vmem, vmem, vmem),
         scratch_shapes=[
+            pltpu.VMEM((rows, LANES), jnp.int32),
             pltpu.VMEM((steps, 2 * SPLIT, rows, LANES), jnp.float32),
             pltpu.VMEM((steps, 2 * SPLIT, rows, LANES), jnp.float32),
             pltpu.VMEM((SPLIT + 1, frames, rows, LANES), jnp.float32),
         ],
         compiler_params=pltpu.CompilerParams(vmem_limit_bytes=60 * 1024 * 1024),
         name="lattice",
-    )(lax.axis_index("seq").reshape(1), gathered, meta, logprob, flat_rows, out_weight)
-    batch_total = utterances * lax.axis_size("dp")
-    partial_sum = lax.psum_scatter(term / batch_total, "dp", scatter_dimension=0, tiled=True)
-    weight_grad = lax.psum_scatter(partial_sum, "seq", scatter_dimension=1, tiled=True)
+    )(label_count, frame_count, gathered, labels, logprob, flat_rows, out_weight)
+    weight_grad = reduce_terms(term, utterances * dp_count)
     return (
         logit_grad.reshape(utterances, frames, vocabulary),
         row_grad.reshape(utterances, frames, width),

time: 147 us -> 59.6 us (0.41)
  waiting for transfers between devices: 94.7 us -> 0 us
  Pallas kernels: 30 us -> 56.4 us
  between operations: 14.1 us -> 0.65 us
  other arithmetic: 4.81 us -> 0 us
    reduce_scatter x2 -> x0, waiting for transfers between devices: 94.7 us -> none  [the longest x1 72.1 us: shards(): lax.psum_scatter(term / batch_total, 'dp', scatter_dimension=0, tiled=True)]
    pallas_call x2 -> x3, Pallas kernels: 30 us -> 56.4 us  [the longest x1 26.1 us: reduce_terms(): pl.pallas_call(functools.partial(reduce_kernel, seq_count, dp_count, batc...]
    div x1 -> x0, other arithmetic: 3.55 us -> none  [shards(): term / batch_total]
    unnamed x0 -> x3, local copies, waits for them, and re-layouts: none -> 2.38 us
    another operation x5 -> x0, local copies, waits for them, and re-layouts: 2.22 us -> none  [the longest x3 2.13 us: shards(): jnp.stack([padded, jnp.broadcast_to(label_count[:, None], (utterances, LA...]
  transfers between devices with their start and end apart: 2 -> 0, of which waited for: 2 -> 0; matrix products, arithmetic and copies ran while one was open for 0% -> 0% of each run, Pallas kernels for 0% -> 0%
where the time goes in v2:
time: 59.6 us; the launch traced here: 59.4 us
  Pallas kernels  56.4 us (95%)
  local copies, waits for them, and re-layouts  2.38 us (4%)
  between operations  0.65 us (1%)
    pallas_call x1, Pallas kernels, reduce_terms(): pl.pallas_call(functools.partial(reduce_kernel, seq_count, dp_count, batc...  26.1 us
    pallas_call x1, Pallas kernels, shards(): pl.pallas_call(lattice_kernel, out_shape=(jax.ShapeDtypeStruct((utterance...  20.9 us
    pallas_call x1, Pallas kernels, shards(): pl.pallas_call(functools.partial(emission_kernel, seq_count), out_shape=(...  9.39 us
    unnamed x3, local copies, waits for them, and re-layouts  2.38 us

profile of v2, /device:TPU:0, one launch (start us, length us, event | category | flops | bytes accessed | tf_op | source)
XLA Modules:
  0.0 59.4 jit_solution(9859453445957753393)
XLA Ops:
  0.6 9.4 %emission.1 = (f32[256,512]{1,0:T(8,128)}, f32[4,2,64,128]{3,2,1,0:T(8,128)}) custom-call(bf16[256,1280]{1,0:T(8,128)(2,1)} %bitcast.5, bf16[1280,512]{1,0:T(8,128)(2,1)} %weight_ref.3, s32[4,63]{1,0:T(4,128)} %labels_ref.3), custom_call_target="tpu_custom_call" | custom-call | tf_op jit(solution)/shard_map/emission/pallas_call | solution.py:387
  10.0 20.9 %lattice.1 = (bf16[256,512]{1,0:T(8,128)(2,1)}, bf16[256,1280]{1,0:T(8,128)(2,1)}, f32[4,8,160,128]{3,2,1,0:T(8,128)}) custom-call(s32[4]{0:T(128)} %label_count_ref.1, s32[4]{0:T(128)} %frame_count_ref.1, f32[4,2,64,128]{3,2,1,0:T(8,128)} %get-tuple-element.8.gathered_ref, s32[4,63]{1,0:T(4,128)} %labels_ref.3, f32[256,512]{1,0:T(8,128)} %get-tuple-element.9.logprob_ref, ...), custom_call_target="tpu_custom_call" | custom-call | tf_op jit(solution)/shard_map/lattice/pallas_call | solution.py:408
  31.0 0.0 copy-start
  31.0 1.7 %copy-done = f32[4,8,160,128]{3,2,1,0:T(8,128)S(1)} copy-done((f32[4,8,160,128]{3,2,1,0:T(8,128)S(1)}, f32[4,8,160,128]{3,2,1,0:T(8,128)}, u32[]{:S(2)}) %copy-start) | copy-done | bytes 2621464
  32.7 26.1 %reduce.1 = f32[160,128]{1,0:T(8,128)S(1)} custom-call(f32[2,2,2,2,2,160,128]{6,5,4,3,2,1,0:T(8,128)S(1)} %bitcast.4), custom_call_target="tpu_custom_call" | custom-call | tf_op jit(solution)/shard_map/reduce/pallas_call | solution.py:363
  58.8 0.6 %copy.9 = f32[160,128]{1,0:T(8,128)} copy(f32[160,128]{1,0:T(8,128)S(1)} %reduce.1) | data formatting | bytes 163840
Async XLA Ops:
  31.0 1.7 %copy-start = (f32[4,8,160,128]{3,2,1,0:T(8,128)S(1)}, f32[4,8,160,128]{3,2,1,0:T(8,128)}, u32[]{:S(2)}) copy-start(f32[4,8,160,128]{3,2,1,0:T(8,128)} %get-tuple-element.12) | copy-start | bytes 7864324

commit v3 on v2

--- a/solution.py
+++ b/solution.py
@@ -9,8 +9,8 @@
 
 negative_fill = -1e30
 LANES = 128
-SPLIT = 2
-UNROLL = 16
+SPLIT = 4
+UNROLL = 32
 MESH = pl.DeviceIdType.MESH
 BOTH_LAST = (((1,), (1,)), ((), ()))
 
@@ -31,14 +31,10 @@
     return table_ref[...]
 
 
-def emission_kernel(seq_count, enc_ref, weight_ref, labels_ref,
-                    logprob_ref, gathered_ref, table_ref, send_sems, recv_sems):
+def share_emissions(seq_count, enc_ref, weight_ref, labels_ref,
+                    logprob_ref, gathered_ref, table_ref, send_sems, recv_sems, before_sending):
     utterances, length = labels_ref.shape
     me = lax.axis_index("seq")
-    barrier = pltpu.get_barrier_semaphore()
-    for step in range(1, seq_count):
-        peer = lax.rem(me + step, seq_count)
-        pl.semaphore_signal(barrier, inc=1, device_id={"seq": peer}, device_id_type=MESH)
     frames = enc_ref.shape[0] // utterances
     vocabulary = weight_ref.shape[1]
     groups = gathered_ref.shape[1]
@@ -66,7 +62,7 @@
                 picked += jnp.dot(part, one_hot, preferred_element_type=jnp.float32)
         gathered_ref[me, group] = picked
     logprob_ref[...] = logprob
-    pl.semaphore_wait(barrier, seq_count - 1)
+    before_sending()
     copies = []
     for step in range(1, seq_count):
         peer = lax.rem(me + step, seq_count)
@@ -95,9 +91,8 @@
     return values
 
 
-def lattice_kernel(label_count_ref, frame_count_ref, gathered_ref, labels_ref, logprob_ref, enc_ref,
-                   weight_ref, logit_ref, row_ref, term_ref, table_ref, level_ref, factor_ref,
-                   mass_ref):
+def lattice_gradients(label_count_ref, frame_count_ref, gathered_ref, labels_ref, logprob_ref,
+                      logit_ref, table_ref, level_ref, factor_ref, mass_ref):
     utterances, length = labels_ref.shape
     seq_count, groups, frames = gathered_ref.shape[:3]
     steps = seq_count * frames
@@ -261,16 +256,6 @@
         own = slice(u * frames, (u + 1) * frames)
         kept = jnp.where(times < frame_count_ref[u], jnp.exp(logprob_ref[own, :]) - mass, 0.0)
         logit_ref[own, :] = kept.astype(jnp.bfloat16)
-    grad = logit_ref[...]
-    row_ref[...] = lax.dot_general(
-        grad, weight_ref[...], BOTH_LAST, preferred_element_type=jnp.float32
-    ).astype(jnp.bfloat16)
-    seq_blocks, dp_blocks, block_rows, block_columns = term_ref.shape
-    for s in range(seq_blocks):
-        term_ref[s] = lax.dot_general(
-            enc_ref[...], grad[:, s * block_columns:(s + 1) * block_columns],
-            (((0,), (0,)), ((), ())), preferred_element_type=jnp.float32,
-        ).reshape(dp_blocks, block_rows, block_columns)
 
 
 def binary_digits(axis, count):
@@ -290,7 +275,7 @@
     first, others = seq_bits[:1], seq_bits[1:]
     along = first + others + dp_bits
     across = first + dp_bits[:1] + others + dp_bits[1:]
-    held = seq_bits[::-1] + dp_bits[::-1]
+    held = others[::-1] + dp_bits[::-1]
     return held, (along, across)
 
 
@@ -299,78 +284,96 @@
     return [(low, min(quarter, rows - low)) for low in range(0, rows, quarter)]
 
 
-def reduce_kernel(seq_count, dp_count, batch_total, term_ref, out_ref, *scratch):
+def fused_kernel(seq_count, dp_count, label_count_ref, frame_count_ref, enc_ref, weight_ref,
+                 labels_ref, logit_ref, row_ref, out_ref, logprob_ref, gathered_ref, table_ref,
+                 level_ref, factor_ref, mass_ref, sent_ref, kept_ref, share_send, share_recv,
+                 send_sems, recv_sems, *landed):
+    me = lax.axis_index("seq")
     digits = {
         (axis, i): entry
         for axis, count in (("seq", seq_count), ("dp", dp_count))
         for i, entry in enumerate(binary_digits(axis, count))
     }
+    greeted = [("seq", lax.rem(me + step, seq_count)) for step in range(1, seq_count)]
+    greeted += [(axis, partner) for axis, _, partner in digits.values() if axis == "dp"]
     barrier = pltpu.get_barrier_semaphore()
-    for axis, digit, partner in digits.values():
+    for axis, partner in greeted:
         pl.semaphore_signal(barrier, inc=1, device_id={axis: partner}, device_id_type=MESH)
-    pl.semaphore_wait(barrier, len(digits))
+
+    def before_sending():
+        pl.semaphore_wait(barrier, len(greeted))
+
+    share_emissions(seq_count, enc_ref, weight_ref, labels_ref, logprob_ref, gathered_ref,
+                    table_ref, share_send, share_recv, before_sending)
+    lattice_gradients(label_count_ref, frame_count_ref, gathered_ref, labels_ref, logprob_ref,
+                      logit_ref, table_ref, level_ref, factor_ref, mass_ref)
+
+    grad = logit_ref[...]
+    columns = sent_ref.shape[-1]
+    core = digits[("seq", 0)][1]
+    even = [grad[:, s * columns:(s + 1) * columns] for s in range(0, seq_count, 2)]
+    odd = [grad[:, s * columns:(s + 1) * columns] for s in range(1, seq_count, 2)]
+
+    def fill(target_ref, halves):
+        product = lax.dot_general(
+            enc_ref[...], jnp.concatenate(halves, axis=1), (((0,), (0,)), ((), ())),
+            preferred_element_type=jnp.float32,
+        )
+        high = (seq_count // 2).bit_length() - 1
+        for h in range(seq_count // 2):
+            place = tuple((h >> (high - 1 - i)) & 1 for i in range(high))
+            piece = product[:, h * columns:(h + 1) * columns]
+            target_ref[place] = piece.reshape(target_ref.shape[high:])
+
+    first = core == 0
+    fill(sent_ref, [jnp.where(first, o, e) for e, o in zip(even, odd)])
+
     held, orders = halving_plan(seq_count, dp_count)
-    chunks = row_chunks(term_ref.shape[-2])
-    stages = len(held)
-    send_sems, recv_sems = scratch[-2:]
-    landing = [scratch[c * stages:(c + 1) * stages] for c in range(len(chunks))]
-    current = [term_ref.at[(slice(None),) * stages + (pl.ds(low, size),)] for low, size in chunks]
+    rows = out_ref.shape[0]
+    chunks = row_chunks(rows)
+    stages = len(held) + 1
+    landing = [landed[c * stages:(c + 1) * stages] for c in range(len(chunks))]
     names = [list(held) for _ in chunks]
     pending = [None] * len(chunks)
 
-    def finish(c, stage):
-        copy, kept = pending[c]
-        copy.wait()
-        target = landing[c][stage]
-        target[...] += kept[...]
-        current[c] = target
-
-    for stage in range(stages):
+    def dense(ref, low, size):
+        return ref.at[(slice(None),) * len(held) + (pl.ds(low, size),)]
+
+    def launch(c, stage, source, kept, bit):
+        axis, _, partner = digits[bit]
+        copy = pltpu.make_async_remote_copy(
+            src_ref=source,
+            dst_ref=landing[c][stage],
+            send_sem=send_sems.at[c, stage],
+            recv_sem=recv_sems.at[c, stage],
+            device_id={axis: partner},
+            device_id_type=MESH,
+        )
+        copy.start()
+        pending[c] = (copy, kept)
+
+    for c, (low, size) in enumerate(chunks):
+        launch(c, 0, dense(sent_ref, low, size), dense(kept_ref, low, size), ("seq", 0))
+    fill(kept_ref, [jnp.where(first, e, o) for e, o in zip(even, odd)])
+    row_ref[...] = lax.dot_general(
+        grad, weight_ref[...], BOTH_LAST, preferred_element_type=jnp.float32
+    ).astype(jnp.bfloat16)
+    for stage in range(1, stages):
         for c in range(len(chunks)):
-            if stage:
-                finish(c, stage - 1)
+            copy, kept = pending[c]
+            copy.wait()
+            current = landing[c][stage - 1]
+            current[...] += kept[...]
             bit = orders[c % 2][stage]
-            position = names[c].index(bit)
+            ahead = (slice(None),) * names[c].index(bit)
             names[c].remove(bit)
-            axis, digit, partner = digits[bit]
-            ahead = (slice(None),) * position
-            copy = pltpu.make_async_remote_copy(
-                src_ref=current[c].at[ahead + (1 - digit,)],
-                dst_ref=landing[c][stage],
-                send_sem=send_sems.at[c, stage],
-                recv_sem=recv_sems.at[c, stage],
-                device_id={axis: partner},
-                device_id_type=MESH,
-            )
-            copy.start()
-            pending[c] = (copy, current[c].at[ahead + (digit,)])
+            digit = digits[bit][1]
+            launch(c, stage, current.at[ahead + (1 - digit,)], current.at[ahead + (digit,)], bit)
     for c, (low, size) in enumerate(chunks):
         copy, kept = pending[c]
         copy.wait()
-        out_ref[low:low + size] = (landing[c][stages - 1][...] + kept[...]) / batch_total
-
-
-def reduce_terms(term, batch_total):
-    seq_count, dp_count, rows, columns = term.shape
-    held, orders = halving_plan(seq_count, dp_count)
-    stages = len(held)
-    chunks = row_chunks(rows)
-    scratch = []
-    for low, size in chunks:
-        for stage in range(stages):
-            scratch.append(pltpu.VMEM((2,) * (stages - 1 - stage) + (size, columns), jnp.float32))
-    vmem = pl.BlockSpec(memory_space=pltpu.VMEM)
-    return pl.pallas_call(
-        functools.partial(reduce_kernel, seq_count, dp_count, batch_total),
-        out_shape=jax.ShapeDtypeStruct((rows, columns), jnp.float32),
-        in_specs=[vmem],
-        out_specs=vmem,
-        scratch_shapes=scratch + [pltpu.SemaphoreType.DMA((len(chunks), stages))] * 2,
-        compiler_params=pltpu.CompilerParams(
-            collective_id=1, has_side_effects=True, vmem_limit_bytes=40 * 1024 * 1024
-        ),
-        name="reduce",
-    )(term.reshape((2,) * stages + (rows, columns)))
+        total = landing[c][stages - 1][...] + kept[...]
+        out_ref[low:low + size] = total / (dp_count * labels_ref.shape[0])
 
 
 def shards(enc_rows, out_weight, labels, label_count, frame_count):
@@ -384,48 +387,47 @@
     flat_rows = enc_rows.reshape(utterances * frames, width)
     vmem = pl.BlockSpec(memory_space=pltpu.VMEM)
 
-    logprob, gathered = pl.pallas_call(
-        functools.partial(emission_kernel, seq_count),
-        out_shape=(
-            jax.ShapeDtypeStruct((utterances * frames, vocabulary), jnp.float32),
-            jax.ShapeDtypeStruct((seq_count, groups, frames, LANES), jnp.float32),
-        ),
-        in_specs=[vmem] * 3,
-        out_specs=(vmem, vmem),
-        scratch_shapes=[
-            pltpu.VMEM((2 * utterances, LANES), jnp.int32),
-            pltpu.SemaphoreType.DMA((seq_count - 1,)),
-            pltpu.SemaphoreType.DMA((seq_count - 1,)),
-        ],
-        compiler_params=pltpu.CompilerParams(collective_id=0, has_side_effects=True),
-        name="emission",
-    )(flat_rows, out_weight, labels)
-
     rows = 2 * utterances
     steps = seq_count * frames
     dp_count = lax.axis_size("dp")
+    held = halving_plan(seq_count, dp_count)[0]
+    block_rows, block_columns = width // dp_count, vocabulary // seq_count
+    whole_block = (2,) * len(held) + (block_rows, block_columns)
+    chunks = row_chunks(block_rows)
+    landed = [
+        pltpu.VMEM((2,) * (len(held) - stage) + (size, block_columns), jnp.float32)
+        for low, size in chunks
+        for stage in range(len(held) + 1)
+    ]
     smem = pl.BlockSpec(memory_space=pltpu.SMEM)
-    logit_grad, row_grad, term = pl.pallas_call(
-        lattice_kernel,
+    logit_grad, row_grad, weight_grad = pl.pallas_call(
+        functools.partial(fused_kernel, seq_count, dp_count),
         out_shape=(
             jax.ShapeDtypeStruct((utterances * frames, vocabulary), jnp.bfloat16),
             jax.ShapeDtypeStruct((utterances * frames, width), jnp.bfloat16),
-            jax.ShapeDtypeStruct(
-                (seq_count, dp_count, width // dp_count, vocabulary // seq_count), jnp.float32
-            ),
+            jax.ShapeDtypeStruct((block_rows, block_columns), jnp.float32),
         ),
-        in_specs=[smem, smem] + [vmem] * 5,
+        in_specs=[smem, smem] + [vmem] * 3,
         out_specs=(vmem, vmem, vmem),
         scratch_shapes=[
+            pltpu.VMEM((utterances * frames, vocabulary), jnp.float32),
+            pltpu.VMEM((seq_count, groups, frames, LANES), jnp.float32),
             pltpu.VMEM((rows, LANES), jnp.int32),
             pltpu.VMEM((steps, 2 * SPLIT, rows, LANES), jnp.float32),
             pltpu.VMEM((steps, 2 * SPLIT, rows, LANES), jnp.float32),
             pltpu.VMEM((SPLIT + 1, frames, rows, LANES), jnp.float32),
-        ],
-        compiler_params=pltpu.CompilerParams(vmem_limit_bytes=60 * 1024 * 1024),
-        name="lattice",
-    )(label_count, frame_count, gathered, labels, logprob, flat_rows, out_weight)
-    weight_grad = reduce_terms(term, utterances * dp_count)
+            pltpu.VMEM(whole_block, jnp.float32),
+            pltpu.VMEM(whole_block, jnp.float32),
+            pltpu.SemaphoreType.DMA((seq_count - 1,)),
+            pltpu.SemaphoreType.DMA((seq_count - 1,)),
+            pltpu.SemaphoreType.DMA((len(chunks), len(held) + 1)),
+            pltpu.SemaphoreType.DMA((len(chunks), len(held) + 1)),
+        ] + landed,
+        compiler_params=pltpu.CompilerParams(
+            collective_id=0, has_side_effects=True, vmem_limit_bytes=60 * 1024 * 1024
+        ),
+        name="fused",
+    )(label_count, frame_count, flat_rows, out_weight, labels)
     return (
         logit_grad.reshape(utterances, frames, vocabulary),
         row_grad.reshape(utterances, frames, width),

time: 59.6 us -> 54.4 us (0.913)
  Pallas kernels: 56.4 us -> 49.2 us
  local copies, waits for them, and re-layouts: 2.38 us -> 4.31 us
    pallas_call x3 -> x1, Pallas kernels: 56.4 us -> 49.2 us  [shards(): pl.pallas_call(functools.partial(fused_kernel, seq_count, dp_count), out_...]
    unnamed x3 -> x5, local copies, waits for them, and re-layouts: 2.38 us -> 4.31 us
where the time goes in v3:
time: 54.4 us; the launch traced here: 54.1 us
  Pallas kernels  49.2 us (90%)
  local copies, waits for them, and re-layouts  4.31 us (8%)
  between operations  0.65 us (1%)
    pallas_call x1, Pallas kernels, shards(): pl.pallas_call(functools.partial(fused_kernel, seq_count, dp_count), out_...  49.2 us
    unnamed x5, local copies, waits for them, and re-layouts  4.31 us

profile of v3, /device:TPU:0, one launch (start us, length us, event | category | flops | bytes accessed | tf_op | source)
XLA Modules:
  0.0 54.1 jit_solution(3133349180444450470)
XLA Ops:
  0.6 49.2 %fused.1 = (bf16[256,512]{1,0:T(8,128)(2,1)}, bf16[256,1280]{1,0:T(8,128)(2,1)}, f32[160,128]{1,0:T(8,128)}) custom-call(s32[4]{0:T(128)} %label_count_ref.1, s32[4]{0:T(128)} %frame_count_ref.1, bf16[256,1280]{1,0:T(8,128)(2,1)} %bitcast.3, bf16[1280,512]{1,0:T(8,128)(2,1)} %weight_ref.1, s32[4,63]{1,0:T(4,128)} %labels_ref.1), custom_call_target="tpu_custom_call" | custom-call | tf_op jit(solution)/shard_map/fused/pallas_call | solution.py:403
  49.8 0.0 copy-start
  49.8 1.7 %copy.11 = bf16[4,64,512]{2,1,0:T(8,128)(2,1)} copy(bf16[4,64,512]{2,1,0:T(8,128)(2,1)} %bitcast.5) | data formatting | bytes 524288
  51.5 2.0 %copy.12 = bf16[4,64,1280]{2,1,0:T(8,128)(2,1)} copy(bf16[4,64,1280]{2,1,0:T(8,128)(2,1)} %bitcast.4) | data formatting | bytes 1310720
  53.5 0.0 copy-done
  53.5 0.6 %copy.13 = f32[160,128]{1,0:T(8,128)} copy(f32[160,128]{1,0:T(8,128)S(1)} %copy-done) | data formatting | bytes 163840
Async XLA Ops:
  49.8 3.7 %copy-start = (f32[160,128]{1,0:T(8,128)S(1)}, f32[160,128]{1,0:T(8,128)}, u32[]{:S(2)}) copy-start(f32[160,128]{1,0:T(8,128)} %get-tuple-element.14) | copy-start | bytes 245764

commit v4 on v3

--- a/solution.py
+++ b/solution.py
@@ -280,7 +280,7 @@
 
 
 def row_chunks(rows):
-    quarter = -(-rows // 4 // 8) * 8
+    quarter = -(-rows // 10 // 8) * 8
     return [(low, min(quarter, rows - low)) for low in range(0, rows, quarter)]
 
 

time: 54.4 us -> 53.6 us (0.985)
  Pallas kernels: 49.2 us -> 48.4 us
    pallas_call x1, Pallas kernels: 49.2 us -> 48.4 us  [shards(): pl.pallas_call(functools.partial(fused_kernel, seq_count, dp_count), out_...]
where the time goes in v4:
time: 53.6 us; the launch traced here: 53.4 us
  Pallas kernels  48.4 us (90%)
  local copies, waits for them, and re-layouts  4.31 us (8%)
  between operations  0.65 us (1%)
    pallas_call x1, Pallas kernels, shards(): pl.pallas_call(functools.partial(fused_kernel, seq_count, dp_count), out_...  48.4 us
    unnamed x5, local copies, waits for them, and re-layouts  4.31 us

profile of v4, /device:TPU:0, one launch (start us, length us, event | category | flops | bytes accessed | tf_op | source)
XLA Modules:
  0.0 53.4 jit_solution(3007658215040116169)
XLA Ops:
  0.6 48.4 %fused.1 = (bf16[256,512]{1,0:T(8,128)(2,1)}, bf16[256,1280]{1,0:T(8,128)(2,1)}, f32[160,128]{1,0:T(8,128)}) custom-call(s32[4]{0:T(128)} %label_count_ref.1, s32[4]{0:T(128)} %frame_count_ref.1, bf16[256,1280]{1,0:T(8,128)(2,1)} %bitcast.3, bf16[1280,512]{1,0:T(8,128)(2,1)} %weight_ref.1, s32[4,63]{1,0:T(4,128)} %labels_ref.1), custom_call_target="tpu_custom_call" | custom-call | tf_op jit(solution)/shard_map/fused/pallas_call | solution.py:403
  49.0 0.0 copy-start
  49.0 1.7 %copy.11 = bf16[4,64,512]{2,1,0:T(8,128)(2,1)} copy(bf16[4,64,512]{2,1,0:T(8,128)(2,1)} %bitcast.5) | data formatting | bytes 524288
  50.8 2.0 %copy.12 = bf16[4,64,1280]{2,1,0:T(8,128)(2,1)} copy(bf16[4,64,1280]{2,1,0:T(8,128)(2,1)} %bitcast.4) | data formatting | bytes 1310720
  52.7 0.0 copy-done
  52.7 0.6 %copy.13 = f32[160,128]{1,0:T(8,128)} copy(f32[160,128]{1,0:T(8,128)S(1)} %copy-done) | data formatting | bytes 163840
Async XLA Ops:
  49.0 3.7 %copy-start = (f32[160,128]{1,0:T(8,128)S(1)}, f32[160,128]{1,0:T(8,128)}, u32[]{:S(2)}) copy-start(f32[160,128]{1,0:T(8,128)} %get-tuple-element.14) | copy-start | bytes 245764
